TPU v7x, 256 devices: a whole 4x4x8 slice. The times are simulated.
256 devices in a mesh: gx: 32 (over x, z_hi, y), vz: 8 (over z_lo, core).
Axes of the slice: x: 4, y: 4, z: 8 (z_hi: 2, z_lo: 4; z = z_hi * 4 + z_lo), core: 2. Of those that a mesh axis runs over, the one named last changes fastest.
Arguments:
- density: float32 [24, 256, 64, 256], P('vz', 'gx'), may hold values from 0.02 to 2.5, as said below
- shift_depth: int32 [16], replicated, may hold values from -20 to 20, as said below
- sub_cell: float32 [16], replicated, may hold values from 0 to 1
- gravity_kick: float32 [256, 64], P('gx'), may hold values from -0.9 to 0.9
- collision: float32 [256, 64], P('gx'), may hold values from 0.1 to 10
Outputs:
- relaxed: float32 [24, 256, 64, 256], P('vz', 'gx')
Inputs may be any that keep to these rules, and one draw needn't show every extreme that they name: `density`: every value is positive. `shift_depth`: some x velocity has 20 and some has -20.
All inputs are finite; a program needn't handle non-finite values.
Results may differ from a plain program's by a relative error of at most 0.00002.
Values sent between devices are 32-bit elements; how exact they have to be, the bound alone decides.
A program may use at most 64 MiB of HBM per device.

v0:
```python
import jax
import jax.numpy as jnp
from jax import lax
from jax.sharding import Mesh
from jax.sharding import PartitionSpec as P

NVX = 16
NVY = 16
VZ = ("vz_0", "vz_1")


def grouped_exchange(x, axis, split_dim, concat_dim, work, item_dim, out_dim):

    def moved(group):
        return lax.all_to_all(group, axis, split_axis=split_dim, concat_axis=concat_dim, tiled=True)

    items = jax.tree.leaves(x)[0].shape[item_dim]
    ends = [items * k // 2 for k in range(2 + 1)] if items % 2 == 0 else [0, items]
    groups = [
        jax.tree.map(lambda a: lax.slice_in_dim(a, low, high, axis=item_dim), x)
        for low, high in zip(ends, ends[1:])
    ]
    arrived = [moved(group) for group in groups]
    made = [work(group) for group in arrived]
    return jax.tree.map(lambda *parts: jnp.concatenate(parts, axis=out_dim), *made)


def padded_2(cells, sides, width):
    for axis, dim in sides:
        count = lax.axis_size(axis)
        ends = count - 1
        head = lax.slice_in_dim(cells, 0, width, axis=dim)
        tail = lax.slice_in_dim(cells, cells.shape[dim] - width, cells.shape[dim], axis=dim)
        cells = jnp.concatenate(
            [
                lax.ppermute(tail, axis, [(i, (i + 1) % count) for i in range(ends)]),
                cells,
                lax.ppermute(head, axis, [((i + 1) % count, i) for i in range(ends)]),
            ],
            axis=dim,
        )
    return cells


def one_axis_at_a_time(x, axes):
    for axis in axes:
        x = lax.psum(x, axis)
    return x


def velocity_values(indices, count, extent):
    return (indices.astype(jnp.float32) - (count - 1) / 2.0) * (extent / count)


def shift_groups(source, starts_near, starts_far, length, sub_cell, axis_x):
    lead = source.shape[:-1]
    grouped = source.reshape(lead + (NVX, NVY))
    pieces = []
    for group in range(NVX):
        column_set = lax.index_in_dim(grouped, group, axis=len(lead), keepdims=False)
        near = lax.dynamic_slice_in_dim(column_set, starts_near[group], length, axis_x)
        far = lax.dynamic_slice_in_dim(column_set, starts_far[group], length, axis_x)
        pieces.append((1.0 - sub_cell[group]) * near + sub_cell[group] * far)
    joined = jnp.stack(pieces, axis=len(lead))
    out_lead = joined.shape[: len(lead)]
    return joined.reshape(out_lead + (NVX * NVY,))


def per_device(density, shift_depth, sub_cell, gravity_kick, collision):
    slab_planes, strip_cols, rows_y, pairs = density.shape
    slab_count = lax.axis_size(VZ)
    total_vz = slab_planes * slab_count
    speed_x = jnp.repeat(velocity_values(jnp.arange(NVX, dtype=jnp.int32), NVX, 9.0), NVY)
    speed_y = jnp.tile(velocity_values(jnp.arange(NVY, dtype=jnp.int32), NVY, 9.0), NVX)
    plane_ids = lax.axis_index(VZ) * slab_planes + jnp.arange(slab_planes, dtype=jnp.int32)
    speed_z = velocity_values(plane_ids, total_vz, 9.6)
    measure_element = 9.0 / NVX * (9.0 / NVY) * (9.6 / total_vz)

    def advect_columns(block):
        width_x = block.shape[1]
        doubled = jnp.concatenate([block, block], axis=1)
        starts_near = jnp.mod(width_x - shift_depth, width_x)
        starts_far = jnp.mod(width_x - shift_depth - 1, width_x)
        shifted = shift_groups(doubled, starts_near, starts_far, width_x, sub_cell, 1)
        return lax.all_to_all(shifted, "gx", split_axis=1, concat_axis=2, tiled=True)

    moved = grouped_exchange(density, "gx", 2, 1, advect_columns, 0, 0)
    padded = padded_2(moved, ((VZ, 0),), 1)
    kick = gravity_kick[None, :, :, None]
    weight_accelerated = (
        (1.0 - jnp.abs(kick)) * moved
        + jnp.maximum(kick, 0.0) * padded[:-2]
        + jnp.maximum(-kick, 0.0) * padded[2:]
    )
    plane_sums = jnp.sum(weight_accelerated, axis=3)
    local_mass = jnp.sum(plane_sums, axis=0)
    local_flow_x = jnp.sum(weight_accelerated * speed_x, axis=(0, 3))
    local_flow_y = jnp.sum(weight_accelerated * speed_y, axis=(0, 3))
    local_flow_z = jnp.sum(plane_sums * speed_z[:, None, None], axis=0)
    energy_terms = speed_x**2 + speed_y**2
    local_energy = jnp.sum(weight_accelerated * energy_terms, axis=(0, 3)) + jnp.sum(
        plane_sums * (speed_z**2)[:, None, None], axis=0
    )
    mass_sum, momentum_x, momentum_y, momentum_z, energy_sum = (
        one_axis_at_a_time(local_mass, VZ),
        one_axis_at_a_time(local_flow_x, VZ),
        one_axis_at_a_time(local_flow_y, VZ),
        one_axis_at_a_time(local_flow_z, VZ),
        one_axis_at_a_time(local_energy, VZ),
    )
    matter_per_cell = measure_element * mass_sum
    flow_x = measure_element * momentum_x / matter_per_cell
    flow_y = measure_element * momentum_y / matter_per_cell
    flow_z = measure_element * momentum_z / matter_per_cell
    speed_sq = flow_x**2 + flow_y**2 + flow_z**2
    motion_warmth = (measure_element * energy_sum - matter_per_cell * speed_sq) / (
        3.0 * matter_per_cell
    )
    deviation_square = (
        (speed_x - flow_x[None, :, :, None]) ** 2
        + (speed_y - flow_y[None, :, :, None]) ** 2
        + (speed_z[:, None, None, None] - flow_z[None, :, :, None]) ** 2
    )
    agitation_width = matter_per_cell * (2.0 * jnp.pi * motion_warmth) ** (-1.5)
    equilibrium_profile = agitation_width[None, :, :, None] * jnp.exp(
        -deviation_square / (2.0 * motion_warmth[None, :, :, None])
    )
    rate = collision[None, :, :, None]
    return (weight_accelerated + rate * equilibrium_profile) / (1.0 + rate)


def solution(mesh):
    torus = Mesh(mesh.devices.reshape(mesh.shape["gx"], 4, 2), ("gx", "vz_0", "vz_1"))
    return jax.shard_map(
        per_device,
        mesh=torus,
        in_specs=(P(VZ, "gx", None, None), P(), P(), P("gx", None), P("gx", None)),
        out_specs=P(VZ, "gx", None, None),
        check_vma=False,
    )
```

profile of v0, /device:TPU:1, one launch (start us, length us, event | category | flops | bytes accessed | tf_op | source)
XLA Modules:
  0.0 214.6 jit_solution(9858659908536691685)
XLA Ops:
  0.0 3.5 %copy.57 = f32[3,8,64,256]{3,1,0,2:T(8,128)} copy(f32[3,8,64,256]{3,2,1,0:T(8,128)} %param.5) | data formatting | bytes 3145728 | tf_op args[0]
  3.5 14.6 %all-to-all-start = ((f32[3,8,64,256]{3,1,0,2:T(8,128)}), f32[3,8,64,256]{3,1,0,2:T(8,128)S(1)}, u32[]{:S(2)}, u32[]{:S(2)}) async-start(f32[3,8,64,256]{3,1,0,2:T(8,128)} %copy.57), calls=%async_computation | async-start | bytes 3145728 | tf_op jit(solution)/shard_map/all_to_all | solution.py:15
  18.1 0.7 fusion.29
  20.1 0.7 fusion.28
  59.7 0.7 fusion.27
  90.3 0.1 copy.85
  90.4 6.6 %concatenate.13 = f32[3,256,2,16,16]{4,3,1,2,0:T(8,128)} reshape(f32[3,32,8,2,256]{4,2,1,3,0:T(8,128)S(1)} %bitcast.69) | data formatting | bytes 3145728 | tf_op jit(solution)/shard_map/concatenate | solution.py:81
  97.1 8.9 %copy.59 = f32[3,256,2,16,16]{1,4,3,2,0:T(8,128)S(1)} copy(f32[3,256,2,16,16]{4,3,1,2,0:T(8,128)} %concatenate.13) | data formatting | bytes 3145728 | tf_op jit(solution)/shard_map/concatenate | solution.py:81
  106.0 0.1 fusion.18
  106.1 0.1 fusion.4
  106.2 0.7 add_dynamic-update-slice_fusion.14
  107.0 0.8 add_dynamic-update-slice_fusion.13
  107.7 0.7 add_dynamic-update-slice_fusion.12
  108.5 0.7 add_dynamic-update-slice_fusion.11
  109.2 0.8 add_dynamic-update-slice_fusion.10
  109.9 0.7 add_dynamic-update-slice_fusion.9
  110.6 0.8 add_dynamic-update-slice_fusion.8
  111.3 0.8 add_dynamic-update-slice_fusion.7
  112.1 0.7 add_dynamic-update-slice_fusion.6
  112.8 0.7 add_dynamic-update-slice_fusion.5
  113.6 0.7 add_dynamic-update-slice_fusion.4
  114.3 0.8 add_dynamic-update-slice_fusion.3
  115.1 0.7 add_dynamic-update-slice_fusion.2
  115.9 0.8 add_dynamic-update-slice_fusion.1
  116.7 0.7 add_dynamic-update-slice_fusion
  117.4 0.8 fusion.21
  118.2 2.1 copy.61
  120.3 11.8 %all-to-all-start.1 = ((f32[3,256,2,256]{3,2,0,1:T(2,128)}), f32[3,256,2,256]{3,2,0,1:T(2,128)S(1)}, u32[]{:S(2)}, u32[]{:S(2)}) async-start(f32[3,256,2,256]{3,2,0,1:T(2,128)} %copy.61), calls=%async_computation.1 | async-start | bytes 3145728 | tf_op jit(solution)/shard_map/all_to_all | solution.py:85
  132.1 0.1 tile.18
  132.2 0.1 broadcast_in_dim.6
  132.3 0.1 reshape.131
  132.3 0.1 copy.66
  132.4 0.1 copy.64
  132.5 0.1 copy.56
  132.6 0.1 copy.68
  132.7 27.6 %all-to-all-done.1 = f32[3,256,2,256]{3,2,0,1:T(2,128)S(1)} async-done(((f32[3,256,2,256]{3,2,0,1:T(2,128)}), f32[3,256,2,256]{3,2,0,1:T(2,128)S(1)}, u32[]{:S(2)}, u32[]{:S(2)}) %all-to-all-start.1) | async-done | bytes 1572896 | tf_op jit(solution)/shard_map/all_to_all | solution.py:85
  160.2 0.1 copy.84
  160.4 0.1 fusion.26
  160.5 16.7 %collective-permute-start.1 = (f32[1,8,64,256]{3,1,2,0:T(8,128)S(1)}, f32[1,8,64,256]{3,1,2,0:T(8,128)S(1)}, u32[]{:S(2)}, u32[]{:S(2)}) collective-permute-start(f32[1,8,64,256]{3,1,2,0:T(8,128)S(1)} %bitcast.71), channel_id=1, source_target_pairs={{1,0},{2,1},{3,2},{4,3},{5,4},{6,5},{7,6},{9,8},{10,9},{11,10},{12... | collective-permute-start | bytes 1572872 | tf_op jit(solution)/shard_map/ppermute | solution.py:38
  177.2 0.9 copy.65
  178.1 3.2 %collective-permute-start = (f32[1,8,64,256]{3,1,2,0:T(8,128)}, f32[1,8,64,256]{3,1,2,0:T(8,128)S(1)}, u32[]{:S(2)}, u32[]{:S(2)}) collective-permute-start(f32[1,8,64,256]{3,1,2,0:T(8,128)} %bitcast.55), channel_id=1, source_target_pairs={{0,1},{1,2},{2,3},{3,4},{4,5},{5,6},{6,7},{8,9},{9,10},{10,11},{11... | collective-permute-start | bytes 1572872 | tf_op jit(solution)/shard_map/ppermute | solution.py:36
  181.3 0.1 copy.80
  181.4 0.2 copy.63
  181.6 3.8 %collective-permute-done.1 = f32[1,8,64,256]{3,1,2,0:T(8,128)S(1)} collective-permute-done((f32[1,8,64,256]{3,1,2,0:T(8,128)S(1)}, f32[1,8,64,256]{3,1,2,0:T(8,128)S(1)}, u32[]{:S(2)}, u32[]{:S(2)}) %collective-permute-start.1) | collective-permute-done | bytes 524320 | tf_op jit(solution)/shard_map/ppermute | solution.py:38
  185.4 2.3 %collective-permute-done = f32[1,8,64,256]{3,1,2,0:T(8,128)S(1)} collective-permute-done((f32[1,8,64,256]{3,1,2,0:T(8,128)}, f32[1,8,64,256]{3,1,2,0:T(8,128)S(1)}, u32[]{:S(2)}, u32[]{:S(2)}) %collective-permute-start) | collective-permute-done | bytes 524320 | tf_op jit(solution)/shard_map/ppermute | solution.py:36
  187.7 1.4 multiply_reduce_fusion
  189.1 0.1 copy.69
  189.2 0.1 copy.70
  189.2 0.1 multiply_reduce_fusion.3
  189.3 0.1 copy.71
  189.4 0.1 copy.72
  189.5 0.1 copy.73
  189.5 0.1 copy.74
  189.6 12.9 %all-reduce = (f32[8,64]{1,0:T(8,128)S(1)}, f32[8,64]{1,0:T(8,128)S(1)}, f32[8,64]{1,0:T(8,128)S(1)}, f32[8,64]{1,0:T(8,128)S(1)}, f32[8,64]{1,0:T(8,128)S(1)}) all-reduce(f32[8,64]{1,0:T(8,128)S(1)} %copy.69, f32[8,64]{1,0:T(8,128)S(1)} %add.335, f32[8,64]{1,0:T(8,128)S(1)} %copy.72, ...), channel_id=1, replica_groups=mesh['gx'=32,'vz_0'=4,'vz_1'=2] {'vz_0'}, use_global_device_ids=true, to_apply=%region_1.2 | all-reduce | flops 2560 | bytes 20480 | tf_op jit(solution)/shard_map/psum | solution.py:47
  202.5 9.0 %all-reduce.1 = (f32[8,64]{1,0:T(8,128)S(1)}, f32[8,64]{1,0:T(8,128)S(1)}, f32[8,64]{1,0:T(8,128)S(1)}, f32[8,64]{1,0:T(8,128)S(1)}, f32[8,64]{1,0:T(8,128)S(1)}) all-reduce(f32[8,64]{1,0:T(8,128)S(1)} %get-tuple-element.12, f32[8,64]{1,0:T(8,128)S(1)} %get-tuple-element.13, ...), channel_id=1, replica_groups=mesh['gx'=32,'vz_0'=4,'vz_1'=2] {'vz_1'}, use_global_device_ids=true, to_apply=%region_2.3 | all-reduce | flops 2560 | bytes 20480 | tf_op jit(solution)/shard_map/psum | solution.py:47
  211.5 0.1 copy.79
  211.6 0.1 copy.78
  211.7 0.1 subtract_multiply_fusion
  211.8 0.1 copy.77
  211.9 0.1 copy.76
  211.9 0.1 copy.75
  212.0 0.2 multiply_add_fusion
  212.2 0.7 add_divide_fusion
  212.9 1.6 copy.81
  (20 shorter events, 0.1 us)
Async XLA Ops:
  3.5 14.6 %copy-start.3 = (s32[16]{0:T(128)S(1)}, s32[16]{0:T(128)}, u32[]{:S(2)}) copy-start(s32[16]{0:T(128)} %param.6) | copy-start | bytes 196
  3.5 56.2 %copy-start = (f32[16]{0:T(128)S(1)}, f32[16]{0:T(128)}, u32[]{:S(2)}) copy-start(f32[16]{0:T(128)} %param.7) | copy-start | bytes 196
  3.5 86.8 %all-to-all-start = ((f32[3,8,64,256]{3,1,0,2:T(8,128)}), f32[3,8,64,256]{3,1,0,2:T(8,128)S(1)}, u32[]{:S(2)}, u32[]{:S(2)}) async-start(f32[3,8,64,256]{3,1,0,2:T(8,128)} %copy.57), calls=%async_computation | async-start | bytes 3145728 | tf_op jit(solution)/shard_map/all_to_all | solution.py:15
  120.3 12.0 %copy-start.2 = (f32[8,64]{1,0:T(8,128)S(1)}, f32[8,64]{1,0:T(8,128)}, u32[]{:S(2)}) copy-start(f32[8,64]{1,0:T(8,128)} %param.8) | copy-start | bytes 6148
  120.3 12.3 %copy-start.1 = (f32[8,64]{1,0:T(8,128)S(1)}, f32[8,64]{1,0:T(8,128)}, u32[]{:S(2)}) copy-start(f32[8,64]{1,0:T(8,128)} %param.9) | copy-start | bytes 6148
  120.3 39.9 %all-to-all-start.1 = ((f32[3,256,2,256]{3,2,0,1:T(2,128)}), f32[3,256,2,256]{3,2,0,1:T(2,128)S(1)}, u32[]{:S(2)}, u32[]{:S(2)}) async-start(f32[3,256,2,256]{3,2,0,1:T(2,128)} %copy.61), calls=%async_computation.1 | async-start | bytes 3145728 | tf_op jit(solution)/shard_map/all_to_all | solution.py:85
  160.5 24.9 %collective-permute-start.1 = (f32[1,8,64,256]{3,1,2,0:T(8,128)S(1)}, f32[1,8,64,256]{3,1,2,0:T(8,128)S(1)}, u32[]{:S(2)}, u32[]{:S(2)}) collective-permute-start(f32[1,8,64,256]{3,1,2,0:T(8,128)S(1)} %bitcast.71), channel_id=1, source_target_pairs={{1,0},{2,1},{3,2},{4,3},{5,4},{6,5},{7,6},{9,8},{10,9},{11,10},{12... | collective-permute-start | bytes 1572872 | tf_op jit(solution)/shard_map/ppermute | solution.py:38
  178.1 9.7 %collective-permute-start = (f32[1,8,64,256]{3,1,2,0:T(8,128)}, f32[1,8,64,256]{3,1,2,0:T(8,128)S(1)}, u32[]{:S(2)}, u32[]{:S(2)}) collective-permute-start(f32[1,8,64,256]{3,1,2,0:T(8,128)} %bitcast.55), channel_id=1, source_target_pairs={{0,1},{1,2},{2,3},{3,4},{4,5},{5,6},{6,7},{8,9},{9,10},{10,11},{11... | collective-permute-start | bytes 1572872 | tf_op jit(solution)/shard_map/ppermute | solution.py:36
where the time goes:
time: 216 us; the launch traced here: 215 us
  between operations  70.4 us (33%)
  starting transfers between devices  46.3 us (21%)
  waiting for transfers between devices  33.7 us (16%)
  local copies, waits for them, and re-layouts  27.8 us (13%)
  blocking collectives  21.9 us (10%)
  other arithmetic  14.6 us (7%)
    all_to_all x1, waiting for transfers between devices, advect_columns(): lax.all_to_all(shifted, 'gx', split_axis=1, concat_axis=2, tiled=True)  27.6 us
    psum x2, blocking collectives, one_axis_at_a_time(): x = lax.psum(x, axis)  21.9 us
    ppermute x1, starting transfers between devices, padded_2(): lax.ppermute(head, axis, [((i + 1) % count, i) for i in range(ends)])  16.7 us
    concatenate x2, local copies, waits for them, and re-layouts, advect_columns(): doubled = jnp.concatenate([block, block], axis=1)  15.6 us
    all_to_all x1, starting transfers between devices, moved(): lax.all_to_all(group, axis, split_axis=split_dim, concat_axis=concat_dim,...  14.6 us
    all_to_all x1, starting transfers between devices, advect_columns(): lax.all_to_all(shifted, 'gx', split_axis=1, concat_axis=2, tiled=True)  11.8 us
    unnamed x15, other arithmetic  11.1 us
  transfers between devices with their start and end apart: 4, of which 3 were waited for; matrix products, arithmetic and copies ran while one was open for 2% of the time, Pallas kernels for 0%

commit v1 on v0

--- a/solution.py
+++ b/solution.py
@@ -44,7 +44,7 @@
 
 def one_axis_at_a_time(x, axes):
     for axis in axes:
-        x = lax.psum(x, axis)
+        x = jnp.sum(lax.all_gather(x, axis), axis=0)
     return x
 
 

time: 216 us -> 270 us (1.25)
  blocking collectives: 21.9 us -> 75.6 us
    all_gather x0 -> x10, blocking collectives: none -> 75.6 us  [one_axis_at_a_time(): x = jnp.sum(lax.all_gather(x, axis), axis=0)]
    psum x2 -> x0, blocking collectives: 21.9 us -> none  [one_axis_at_a_time(): x = lax.psum(x, axis)]
  transfers between devices with their start and end apart: 4 -> 4, of which waited for: 3 -> 3; matrix products, arithmetic and copies ran while one was open for 2% -> 1% of each run, Pallas kernels for 0% -> 0%
where the time goes in v1:
time: 270 us; the launch traced here: 268 us
  blocking collectives  75.6 us (28%)
  between operations  70.4 us (26%)
  starting transfers between devices  46.3 us (17%)
  waiting for transfers between devices  33.7 us (12%)
  local copies, waits for them, and re-layouts  27.7 us (10%)
  other arithmetic  14.6 us (5%)
    all_gather x10, blocking collectives, one_axis_at_a_time(): x = jnp.sum(lax.all_gather(x, axis), axis=0)  75.6 us
    all_to_all x1, waiting for transfers between devices, advect_columns(): lax.all_to_all(shifted, 'gx', split_axis=1, concat_axis=2, tiled=True)  27.6 us
    ppermute x1, starting transfers between devices, padded_2(): lax.ppermute(head, axis, [((i + 1) % count, i) for i in range(ends)])  16.7 us
    concatenate x2, local copies, waits for them, and re-layouts, advect_columns(): doubled = jnp.concatenate([block, block], axis=1)  15.6 us
    all_to_all x1, starting transfers between devices, moved(): lax.all_to_all(group, axis, split_axis=split_dim, concat_axis=concat_dim,...  14.6 us
    all_to_all x1, starting transfers between devices, advect_columns(): lax.all_to_all(shifted, 'gx', split_axis=1, concat_axis=2, tiled=True)  11.8 us
    unnamed x15, other arithmetic  11.1 us
  transfers between devices with their start and end apart: 4, of which 3 were waited for; matrix products, arithmetic and copies ran while one was open for 1% of the time, Pallas kernels for 0%

profile of v1, /device:TPU:1, one launch (start us, length us, event | category | flops | bytes accessed | tf_op | source)
XLA Modules:
  0.0 268.3 jit_solution(3271098140578557144)
XLA Ops:
  0.0 3.5 %copy.77 = f32[3,8,64,256]{3,1,0,2:T(8,128)} copy(f32[3,8,64,256]{3,2,1,0:T(8,128)} %param.5) | data formatting | bytes 3145728 | tf_op args[0]
  3.5 14.6 %all-to-all-start = ((f32[3,8,64,256]{3,1,0,2:T(8,128)}), f32[3,8,64,256]{3,1,0,2:T(8,128)S(1)}, u32[]{:S(2)}, u32[]{:S(2)}) async-start(f32[3,8,64,256]{3,1,0,2:T(8,128)} %copy.77), calls=%async_computation | async-start | bytes 3145728 | tf_op jit(solution)/shard_map/all_to_all | solution.py:15
  18.1 0.7 fusion.29
  20.1 0.7 fusion.28
  59.7 0.7 fusion.27
  90.3 0.1 copy.104
  90.4 6.6 %concatenate.13 = f32[3,256,2,16,16]{4,3,1,2,0:T(8,128)} reshape(f32[3,32,8,2,256]{4,2,1,3,0:T(8,128)S(1)} %bitcast.89) | data formatting | bytes 3145728 | tf_op jit(solution)/shard_map/concatenate | solution.py:81
  97.1 8.9 %copy.79 = f32[3,256,2,16,16]{1,4,3,2,0:T(8,128)S(1)} copy(f32[3,256,2,16,16]{4,3,1,2,0:T(8,128)} %concatenate.13) | data formatting | bytes 3145728 | tf_op jit(solution)/shard_map/concatenate | solution.py:81
  106.0 0.1 fusion.18
  106.1 0.1 fusion.4
  106.2 0.7 add_dynamic-update-slice_fusion.14
  107.0 0.8 add_dynamic-update-slice_fusion.13
  107.7 0.7 add_dynamic-update-slice_fusion.12
  108.5 0.7 add_dynamic-update-slice_fusion.11
  109.2 0.8 add_dynamic-update-slice_fusion.10
  109.9 0.7 add_dynamic-update-slice_fusion.9
  110.6 0.8 add_dynamic-update-slice_fusion.8
  111.3 0.8 add_dynamic-update-slice_fusion.7
  112.1 0.7 add_dynamic-update-slice_fusion.6
  112.8 0.7 add_dynamic-update-slice_fusion.5
  113.6 0.7 add_dynamic-update-slice_fusion.4
  114.3 0.8 add_dynamic-update-slice_fusion.3
  115.1 0.7 add_dynamic-update-slice_fusion.2
  115.9 0.8 add_dynamic-update-slice_fusion.1
  116.7 0.7 add_dynamic-update-slice_fusion
  117.4 0.8 fusion.21
  118.2 2.1 copy.81
  120.3 11.8 %all-to-all-start.1 = ((f32[3,256,2,256]{3,2,0,1:T(2,128)}), f32[3,256,2,256]{3,2,0,1:T(2,128)S(1)}, u32[]{:S(2)}, u32[]{:S(2)}) async-start(f32[3,256,2,256]{3,2,0,1:T(2,128)} %copy.81), calls=%async_computation.1 | async-start | bytes 3145728 | tf_op jit(solution)/shard_map/all_to_all | solution.py:85
  132.1 0.1 tile.18
  132.3 0.1 reshape.191
  132.3 0.1 copy.86
  132.4 0.1 copy.84
  132.5 0.1 copy.76
  132.6 0.1 copy.88
  132.7 27.6 %all-to-all-done.1 = f32[3,256,2,256]{3,2,0,1:T(2,128)S(1)} async-done(((f32[3,256,2,256]{3,2,0,1:T(2,128)}), f32[3,256,2,256]{3,2,0,1:T(2,128)S(1)}, u32[]{:S(2)}, u32[]{:S(2)}) %all-to-all-start.1) | async-done | bytes 1572896 | tf_op jit(solution)/shard_map/all_to_all | solution.py:85
  160.2 0.1 copy.103
  160.5 16.7 %collective-permute-start.1 = (f32[1,8,64,256]{3,1,2,0:T(8,128)S(1)}, f32[1,8,64,256]{3,1,2,0:T(8,128)S(1)}, u32[]{:S(2)}, u32[]{:S(2)}) collective-permute-start(f32[1,8,64,256]{3,1,2,0:T(8,128)S(1)} %bitcast.91), channel_id=1, source_target_pairs={{1,0},{2,1},{3,2},{4,3},{5,4},{6,5},{7,6},{9,8},{10,9},{11,10},{12... | collective-permute-start | bytes 1572872 | tf_op jit(solution)/shard_map/ppermute | solution.py:38
  177.2 0.9 copy.85
  178.1 3.2 %collective-permute-start = (f32[1,8,64,256]{3,1,2,0:T(8,128)}, f32[1,8,64,256]{3,1,2,0:T(8,128)S(1)}, u32[]{:S(2)}, u32[]{:S(2)}) collective-permute-start(f32[1,8,64,256]{3,1,2,0:T(8,128)} %bitcast.55), channel_id=1, source_target_pairs={{0,1},{1,2},{2,3},{3,4},{4,5},{5,6},{6,7},{8,9},{9,10},{10,11},{11... | collective-permute-start | bytes 1572872 | tf_op jit(solution)/shard_map/ppermute | solution.py:36
  181.3 0.1 copy.99
  181.4 0.2 copy.83
  181.6 3.8 %collective-permute-done.1 = f32[1,8,64,256]{3,1,2,0:T(8,128)S(1)} collective-permute-done((f32[1,8,64,256]{3,1,2,0:T(8,128)S(1)}, f32[1,8,64,256]{3,1,2,0:T(8,128)S(1)}, u32[]{:S(2)}, u32[]{:S(2)}) %collective-permute-start.1) | collective-permute-done | bytes 524320 | tf_op jit(solution)/shard_map/ppermute | solution.py:38
  185.4 2.3 collective-permute-done
  187.7 1.4 multiply_reduce_fusion
  189.2 10.3 %all-gather = f32[32,64]{1,0:T(8,128)S(1)} all-gather(f32[8,64]{1,0:T(8,128)S(1)} %copy.89), channel_id=2, replica_groups=mesh['gx'=32,'vz_0'=4,'vz_1'=2] {'vz_0'}, dimensions={0}, use_global_device_ids=true | all-gather | bytes 10240 | tf_op jit(solution)/shard_map/all_gather | solution.py:47
  199.5 5.2 %all-gather.1 = f32[16,64]{1,0:T(8,128)S(1)} all-gather(f32[8,64]{1,0:T(8,128)S(1)} %bitcast_reduce_fusion.4), channel_id=3, replica_groups=mesh['gx'=32,'vz_0'=4,'vz_1'=2] {'vz_1'}, dimensions={0}, use_global_device_ids=true | all-gather | bytes 6144 | tf_op jit(solution)/shard_map/all_gather | solution.py:47
  204.7 0.1 multiply_reduce_fusion.3
  204.9 10.3 %all-gather.8 = f32[32,64]{1,0:T(8,128)S(1)} all-gather(f32[8,64]{1,0:T(8,128)S(1)} %copy.93), channel_id=10, replica_groups=mesh['gx'=32,'vz_0'=4,'vz_1'=2] {'vz_0'}, dimensions={0}, use_global_device_ids=true | all-gather | bytes 10240 | tf_op jit(solution)/shard_map/all_gather | solution.py:47
  215.2 4.7 %all-gather.9 = f32[16,64]{1,0:T(8,128)S(1)} all-gather(f32[8,64]{1,0:T(8,128)S(1)} %bitcast_reduce_fusion), channel_id=11, replica_groups=mesh['gx'=32,'vz_0'=4,'vz_1'=2] {'vz_1'}, dimensions={0}, use_global_device_ids=true | all-gather | bytes 6144 | tf_op jit(solution)/shard_map/all_gather | solution.py:47
  220.0 10.3 %all-gather.6 = f32[32,64]{1,0:T(8,128)S(1)} all-gather(f32[8,64]{1,0:T(8,128)S(1)} %copy.92), channel_id=8, replica_groups=mesh['gx'=32,'vz_0'=4,'vz_1'=2] {'vz_0'}, dimensions={0}, use_global_device_ids=true | all-gather | bytes 10240 | tf_op jit(solution)/shard_map/all_gather | solution.py:47
  230.3 4.7 %all-gather.7 = f32[16,64]{1,0:T(8,128)S(1)} all-gather(f32[8,64]{1,0:T(8,128)S(1)} %bitcast_reduce_fusion.1), channel_id=9, replica_groups=mesh['gx'=32,'vz_0'=4,'vz_1'=2] {'vz_1'}, dimensions={0}, use_global_device_ids=true | all-gather | bytes 6144 | tf_op jit(solution)/shard_map/all_gather | solution.py:47
  235.1 10.3 %all-gather.4 = f32[32,64]{1,0:T(8,128)S(1)} all-gather(f32[8,64]{1,0:T(8,128)S(1)} %copy.91), channel_id=6, replica_groups=mesh['gx'=32,'vz_0'=4,'vz_1'=2] {'vz_0'}, dimensions={0}, use_global_device_ids=true | all-gather | bytes 10240 | tf_op jit(solution)/shard_map/all_gather | solution.py:47
  245.4 4.7 %all-gather.5 = f32[16,64]{1,0:T(8,128)S(1)} all-gather(f32[8,64]{1,0:T(8,128)S(1)} %bitcast_reduce_fusion.2), channel_id=7, replica_groups=mesh['gx'=32,'vz_0'=4,'vz_1'=2] {'vz_1'}, dimensions={0}, use_global_device_ids=true | all-gather | bytes 6144 | tf_op jit(solution)/shard_map/all_gather | solution.py:47
  250.2 10.3 %all-gather.2 = f32[32,64]{1,0:T(8,128)S(1)} all-gather(f32[8,64]{1,0:T(8,128)S(1)} %copy.90), channel_id=4, replica_groups=mesh['gx'=32,'vz_0'=4,'vz_1'=2] {'vz_0'}, dimensions={0}, use_global_device_ids=true | all-gather | bytes 10240 | tf_op jit(solution)/shard_map/all_gather | solution.py:47
  260.5 4.7 %all-gather.3 = f32[16,64]{1,0:T(8,128)S(1)} all-gather(f32[8,64]{1,0:T(8,128)S(1)} %bitcast_reduce_fusion.3), channel_id=5, replica_groups=mesh['gx'=32,'vz_0'=4,'vz_1'=2] {'vz_1'}, dimensions={0}, use_global_device_ids=true | all-gather | bytes 6144 | tf_op jit(solution)/shard_map/all_gather | solution.py:47
  265.2 0.1 copy.98
  265.3 0.1 copy.97
  265.4 0.1 subtract_multiply_fusion
  265.5 0.1 copy.96
  265.6 0.1 copy.95
  265.7 0.1 copy.94
  265.7 0.2 multiply_add_fusion
  266.0 0.7 add_divide_fusion
  266.6 1.6 copy.100
  (37 shorter events, 0.6 us)
Async XLA Ops:
  3.5 14.6 %copy-start.3 = (s32[16]{0:T(128)S(1)}, s32[16]{0:T(128)}, u32[]{:S(2)}) copy-start(s32[16]{0:T(128)} %param.6) | copy-start | bytes 196
  3.5 56.2 %copy-start = (f32[16]{0:T(128)S(1)}, f32[16]{0:T(128)}, u32[]{:S(2)}) copy-start(f32[16]{0:T(128)} %param.7) | copy-start | bytes 196
  3.5 86.8 %all-to-all-start = ((f32[3,8,64,256]{3,1,0,2:T(8,128)}), f32[3,8,64,256]{3,1,0,2:T(8,128)S(1)}, u32[]{:S(2)}, u32[]{:S(2)}) async-start(f32[3,8,64,256]{3,1,0,2:T(8,128)} %copy.77), calls=%async_computation | async-start | bytes 3145728 | tf_op jit(solution)/shard_map/all_to_all | solution.py:15
  120.3 12.0 %copy-start.2 = (f32[8,64]{1,0:T(8,128)S(1)}, f32[8,64]{1,0:T(8,128)}, u32[]{:S(2)}) copy-start(f32[8,64]{1,0:T(8,128)} %param.8) | copy-start | bytes 6148
  120.3 12.3 %copy-start.1 = (f32[8,64]{1,0:T(8,128)S(1)}, f32[8,64]{1,0:T(8,128)}, u32[]{:S(2)}) copy-start(f32[8,64]{1,0:T(8,128)} %param.9) | copy-start | bytes 6148
  120.3 39.9 %all-to-all-start.1 = ((f32[3,256,2,256]{3,2,0,1:T(2,128)}), f32[3,256,2,256]{3,2,0,1:T(2,128)S(1)}, u32[]{:S(2)}, u32[]{:S(2)}) async-start(f32[3,256,2,256]{3,2,0,1:T(2,128)} %copy.81), calls=%async_computation.1 | async-start | bytes 3145728 | tf_op jit(solution)/shard_map/all_to_all | solution.py:85
  160.5 24.9 %collective-permute-start.1 = (f32[1,8,64,256]{3,1,2,0:T(8,128)S(1)}, f32[1,8,64,256]{3,1,2,0:T(8,128)S(1)}, u32[]{:S(2)}, u32[]{:S(2)}) collective-permute-start(f32[1,8,64,256]{3,1,2,0:T(8,128)S(1)} %bitcast.91), channel_id=1, source_target_pairs={{1,0},{2,1},{3,2},{4,3},{5,4},{6,5},{7,6},{9,8},{10,9},{11,10},{12... | collective-permute-start | bytes 1572872 | tf_op jit(solution)/shard_map/ppermute | solution.py:38
  178.1 9.7 %collective-permute-start = (f32[1,8,64,256]{3,1,2,0:T(8,128)}, f32[1,8,64,256]{3,1,2,0:T(8,128)S(1)}, u32[]{:S(2)}, u32[]{:S(2)}) collective-permute-start(f32[1,8,64,256]{3,1,2,0:T(8,128)} %bitcast.55), channel_id=1, source_target_pairs={{0,1},{1,2},{2,3},{3,4},{4,5},{5,6},{6,7},{8,9},{9,10},{10,11},{11... | collective-permute-start | bytes 1572872 | tf_op jit(solution)/shard_map/ppermute | solution.py:36
